TPU v7x, 256 devices: a whole 4x4x8 slice. The times are simulated.
256 devices in a mesh: pole: 4 (over y), row: 8 (over z), col: 8 (over x, core).
Axes of the slice: x: 4, y: 4, z: 8, core: 2. Of those that a mesh axis runs over, the one named last changes fastest.
Arguments:
- root_inverse: float32 [8, 1024, 1024], P('pole', ('row', 'col')), may hold values from -100 to 100
- node_factor: float32 [8, 8, 1024, 512], P('pole', 'row', None, 'col'), may hold values from -0.1875 to 0.1875
- node_inverse: float32 [8, 8, 512, 512], P('pole', 'row'), may hold values from -100 to 100
- leaf_root_factor: float32 [8, 64, 1024, 256], P('pole', ('row', 'col')), may hold values from -0.1875 to 0.1875
- leaf_node_factor: float32 [8, 64, 512, 256], P('pole', ('row', 'col')), may hold values from -0.25 to 0.25
- leaf_inverse: float32 [8, 64, 256, 256], P('pole', ('row', 'col')), may hold values from -100 to 100
- leaf_pattern: int32 [64, 8], P(('row', 'col')), may hold values 0 or 1
- pole_weight: float32 [8], P('pole'), may hold values from 0.1 to 1
Outputs:
- root_block: float32 [1024, 1024], P(('row', 'col'))
- node_offdiag: float32 [8, 1024, 512], P('row', None, 'col')
- node_diag: float32 [8, 512, 512], P('row', 'col')
- leaf_root: float32 [64, 1024, 256], P(('row', 'col'))
- leaf_node: float32 [64, 512, 256], P(('row', 'col'))
- leaf_diag: float32 [64, 256, 256], P(('row', 'col'))
All inputs are finite; a program needn't handle non-finite values. No bound on the sum of `leaf_pattern` on one device may be relied on, other than what follows from the above.
Results may differ from a plain program's by a relative error of at most 0.0001.
Values sent between devices are 32-bit elements; how exact they have to be, the bound alone decides.
A program may use at most 64 MiB of HBM per device.

v0:
```python
import jax
import jax.numpy as jnp
from jax import lax
from jax.sharding import PartitionSpec as P

highest = lax.Precision.HIGHEST


def product(left, right):
    return jnp.matmul(left, right, precision=highest)


def weighted(weights, values):
    return jnp.sum(weights[:, None, None] * values, axis=0)


def shards(
    root_inverse,
    node_factor,
    node_inverse,
    leaf_root_factor,
    leaf_node_factor,
    leaf_inverse,
    leaf_pattern,
    pole_weight,
):
    node_cols = node_factor[:, 0]
    node_inv = node_inverse[:, 0]
    node_leaf = leaf_node_factor[:, 0]
    leaf_inv = leaf_inverse[:, 0]
    block_rows = leaf_root_factor.shape[2] // leaf_pattern.shape[1]
    row_mask = jnp.repeat(leaf_pattern[0].astype(jnp.float32), block_rows)
    root_leaf = leaf_root_factor[:, 0] * row_mask[None, :, None]
    width = node_cols.shape[2]
    joined = jnp.concatenate([node_cols, root_leaf], axis=2)
    products = product(lax.all_gather(root_inverse, ("row", "col"), axis=1, tiled=True), joined)
    offdiag = -products[:, :, :width]
    root_times = products[:, :, width:]
    col_index = lax.axis_index("col")
    own_rows = lax.dynamic_slice_in_dim(node_inv, col_index * width, width, 1)
    factor_t = jnp.swapaxes(node_cols, 1, 2)
    piece = lax.all_gather(offdiag, "col", axis=2, tiled=True)
    root_sum = root_times
    root_sum = root_sum + product(piece, node_leaf)
    node_part = product(jnp.swapaxes(piece, 1, 2), root_leaf)
    cross = product(factor_t, piece)
    root_sum, node_part, cross = (root_sum, node_part, cross)
    diag_rows = own_rows - cross
    diag_times = product(lax.all_gather(diag_rows, "col", axis=1, tiled=True), node_leaf)
    upper_levels = (
        weighted(pole_weight, root_inverse),
        weighted(pole_weight, offdiag)[None],
        weighted(pole_weight, diag_rows)[None],
    )
    middle_part = node_part + diag_times
    lower_part = (
        leaf_inv
        + product(jnp.swapaxes(root_leaf, 1, 2), root_sum)
        + product(jnp.swapaxes(node_leaf, 1, 2), middle_part)
    )
    leaf_levels = (
        weighted(pole_weight, -root_sum)[None],
        weighted(pole_weight, -middle_part)[None],
        weighted(pole_weight, lower_part)[None],
    )
    totals = lax.psum(
        (
            upper_levels[0],
            upper_levels[1],
            upper_levels[2],
            leaf_levels[0],
            leaf_levels[1],
            leaf_levels[2],
        ),
        "pole",
    )
    return (totals[0], totals[1], totals[2], totals[3], totals[4], totals[5])


def solution(mesh):
    return jax.shard_map(
        shards,
        mesh=mesh,
        in_specs=(
            P("pole", ("row", "col"), None),
            P("pole", "row", None, "col"),
            P("pole", "row", None, None),
            P("pole", ("row", "col"), None, None),
            P("pole", ("row", "col"), None, None),
            P("pole", ("row", "col"), None, None),
            P(("row", "col"), None),
            P("pole"),
        ),
        out_specs=(
            P(("row", "col"), None),
            P("row", None, "col"),
            P("row", "col", None),
            P(("row", "col"), None, None),
            P(("row", "col"), None, None),
            P(("row", "col"), None, None),
        ),
        check_vma=False,
    )
```

profile of v0, /device:TPU:1, one launch (start us, length us, event | category | flops | bytes accessed | tf_op | source)
XLA Modules:
  0.0 272.0 jit_solution(6661913665170530114)
XLA Ops:
  7.2 0.0 copy-start
  7.2 0.0 all-gather.4.cloned.1.call-start
  7.2 0.7 all-gather.4.cloned.1.call-update
  7.9 0.0 copy-start.12
  7.9 0.0 all-gather.6.cloned.1.call-start
  8.0 2.9 %copy.20 = f32[2,1,1024,256]{2,3,0,1:T(8,128)} copy(f32[2,1,1024,256]{3,2,1,0:T(8,128)} %param.11) | data formatting | bytes 4194304 | tf_op args[3]
  10.9 0.0 copy-done.12
  10.9 0.1 broadcast_bitcast_fusion
  11.0 1.8 bitcast_multiply_fusion
  12.8 85.2 %all-gather.4.cloned.1.call-done = f32[2,1024,1024]{2,1,0:T(8,128)} async-done(((f32[2,16,1024]{2,1,0:T(8,128)}), f32[2,1024,1024]{2,1,0:T(8,128)}) %all-gather.4.cloned.1.call-update) | async-done | bytes 8388624 | tf_op jit(solution)/shard_map/all_gather | solution.py:36
  98.0 11.3 %fusion.4 = f32[2,1024,320]{1,2,0:T(8,128)S(1)} fusion(f32[2,1024,1024]{2,1,0:T(8,128)} %all-gather.4.cloned.1.call-done, f32[2,1024,256]{1,2,0:T(8,128)S(1)} %bitcast_multiply_fusion, f32[2,1024,64]{1,2,0:T(8,128)} %bitcast.54), kind=kOutput, calls=%fused_computation.7 | convolution fusion | flops 8053719040 | bytes 13631488 | tf_op jit(solution)/shard_map/dot_general | solution.py:10
  109.4 0.0 copy-start.2
  109.4 1.5 copy-done.2
  110.9 0.0 copy-done.11
  110.9 1.6 slice_negate_fusion
  112.5 0.0 all-gather.6.cloned.1.call-update
  112.5 0.0 all-gather.8.cloned.1.call-start
  112.5 0.0 copy-start.6
  112.5 31.9 %all-gather.6.cloned.1.call-done = f32[2,1024,512]{1,2,0:T(8,128)} async-done(((f32[2,1024,64]{1,2,0:T(8,128)}), f32[2,1024,512]{1,2,0:T(8,128)}) %all-gather.6.cloned.1.call-update) | async-done | bytes 4194320 | tf_op jit(solution)/shard_map/all_gather | solution.py:42
  144.5 7.9 %multiply_reduce_fusion.3 = (f32[64,512]{1,0:T(8,128)}, f32[2,64,512]{2,1,0:T(8,128)}) fusion(f32[2]{0:T(128)S(1)} %copy-done.11, f32[2,1024,512]{1,2,0:T(8,128)} %all-gather.6.cloned.1.call-done, f32[2,1,1024,64]{2,3,1,0:T(8,128)} %param.9, f32[2,1,512,512]{3,2,1,0:T(8,128)} %param.10, s32[]{:T(128)S(6)} %select_n.3), kind=kOutput, calls=%fused_computation.23 | convolution fusion | flops 805470208 | bytes 5373964 | tf_op jit(solution)/shard_map/dot_general | solution.py:10
  152.4 0.0 all-gather.8.cloned.1.call-update
  152.4 0.2 all-reduce.3.cloned.1.call-start
  152.6 0.0 copy-done.6
  152.6 0.7 multiply_reduce_fusion.4
  153.3 0.0 copy-done
  153.3 8.0 %multiply_reduce_fusion = (f32[1024,256]{0,1:T(8,128)}, f32[2,1024,256]{1,2,0:T(8,128)S(1)}) fusion(f32[2]{0:T(128)S(1)} %copy-done.11, f32[2,1024,512]{1,2,0:T(8,128)} %all-gather.6.cloned.1.call-done, f32[2,1,512,256]{3,2,1,0:T(8,128)S(1)} %copy-done, f32[2,1024,320]{1,2,0:T(8,128)} %copy-done.2), kind=kOutput, calls=%fused_computation.6 | convolution fusion | flops 3223060480 | bytes 10485768 | tf_op jit(solution)/shard_map/dot_general | solution.py:10
  161.3 0.0 copy-done.4
  161.3 2.9 %convolution_add_fusion.1 = f32[2,256,256]{2,1,0:T(8,128)} fusion(f32[2,1024,256]{1,2,0:T(8,128)S(1)} %bitcast_multiply_fusion, f32[2,1024,256]{1,2,0:T(8,128)S(1)} %get-tuple-element.23, f32[2,1,256,256]{3,2,1,0:T(8,128)S(1)} %copy-done.4), kind=kOutput, calls=%fused_computation.11 | convolution fusion | flops 1610743808 | bytes 5242880 | tf_op jit(solution)/shard_map/dot_general | solution.py:10
  164.2 16.0 %all-gather.8.cloned.1.call-done = f32[2,512,512]{2,1,0:T(8,128)} async-done(((f32[2,64,512]{2,1,0:T(8,128)}), f32[2,512,512]{2,1,0:T(8,128)}) %all-gather.8.cloned.1.call-update) | async-done | bytes 2097168 | tf_op jit(solution)/shard_map/all_gather | solution.py:49
  180.2 3.7 %fusion.12 = f32[2,512,256]{2,1,0:T(8,128)S(1)} fusion(f32[2,512,512]{2,1,0:T(8,128)} %all-gather.8.cloned.1.call-done, f32[2,1,512,256]{3,2,1,0:T(8,128)S(1)} %copy-done), kind=kOutput, calls=%fused_computation.17 | convolution fusion | flops 1610612736 | bytes 4194304 | tf_op jit(solution)/shard_map/dot_general | solution.py:10
  184.0 0.0 copy-done.1
  184.0 0.0 copy-start.3
  184.0 4.7 %multiply_reduce_fusion.1 = (f32[512,256]{1,0:T(8,128)}, f32[2,512,256]{2,1,0:T(8,128)S(1)}) fusion(f32[2]{0:T(128)S(1)} %copy-done.11, f32[2,512,256]{2,1,0:T(8,128)S(1)} %fusion.12, f32[2,1024,512]{1,2,0:T(8,128)S(1)} %copy-done.1, f32[2,1024,256]{1,2,0:T(8,128)S(1)} %bitcast_multiply_fusion), kind=kOutput, calls=%fused_computation.20 | convolution fusion | flops 3222142976 | bytes 8912904 | tf_op jit(solution)/shard_map/dot_general | solution.py:10
  188.6 0.0 copy-done.3
  188.7 2.6 fusion.9
  191.2 0.0 all-reduce.3.cloned.1.call-update
  191.2 68.0 %all-reduce.3.cloned.1.call-done = (f32[16,1024]{1,0:T(8,128)}, f32[1,1024,64]{1,2,0:T(8,128)}, f32[1,64,512]{2,1,0:T(8,128)}, f32[1,1024,256]{1,2,0:T(8,128)}, ...) async-done(((f32[16,1024]{1,0:T(8,128)}, f32[1,1024,64]{1,2,0:T(8,128)}, f32[1,64,512]{2,1,0:T(8,128)}, f32[1,1024,256]{1,2,0:T(8,128)}, f32[1,512,256]{2,1,0:T(8,128)}, ...) | async-done | bytes 2293776 | tf_op jit(solution)/shard_map/psum | solution.py:66
  259.3 2.6 copy.26
  261.9 0.0 copy-done.10
  261.9 0.6 copy.38
  262.6 0.0 copy-done.8
  262.6 0.7 copy.39
  263.3 0.0 copy-done.9
  263.3 0.7 copy.40
  263.9 0.0 copy-done.5
  263.9 0.8 copy.41
  264.7 0.0 copy-done.7
  264.7 0.7 copy.42
  (9 shorter events, 0.0 us)
Async XLA Ops:
  7.2 146.2 %copy-start = (f32[2,1,512,256]{3,2,1,0:T(8,128)S(1)}, f32[2,1,512,256]{3,2,1,0:T(8,128)}, u32[]{:S(2)}) copy-start(f32[2,1,512,256]{3,2,1,0:T(8,128)} %param.12) | copy-start | bytes 3145732
  7.2 90.8 %all-gather.4.cloned.1.call-start = ((), (), s32[]{:S(2)}) async-start(), calls=%async_computation | async-start | bytes 8519680 | tf_op jit(solution)/shard_map/all_gather | solution.py:36
  7.9 3.0 %copy-start.12 = (s32[1,8]{1,0:T(1,128)S(1)}, s32[1,8]{1,0:T(1,128)}, u32[]{:S(2)}) copy-start(s32[1,8]{1,0:T(1,128)} %param.14) | copy-start | bytes 100
  7.9 136.6 %all-gather.6.cloned.1.call-start = ((), (), s32[]{:S(2)}) async-start(), calls=%async_computation.1 | async-start | bytes 4718592 | tf_op jit(solution)/shard_map/all_gather | solution.py:42
  98.0 12.9 %copy-start.11 = (f32[2]{0:T(128)S(1)}, f32[2]{0:T(128)}, u32[]{:S(2)}) copy-start(f32[2]{0:T(128)} %param.15) | copy-start | bytes 28
  109.4 1.5 copy-start.2
  112.5 67.8 %all-gather.8.cloned.1.call-start = ((), (), s32[]{:S(2)}) async-start(), calls=%async_computation.2 | async-start | bytes 2359296 | tf_op jit(solution)/shard_map/all_gather | solution.py:49
  112.5 40.1 %copy-start.6 = (f32[2,16,1024]{2,1,0:T(8,128)S(1)}, f32[2,16,1024]{2,1,0:T(8,128)}, u32[]{:S(2)}) copy-start(f32[2,16,1024]{2,1,0:T(8,128)} %param.8) | copy-start | bytes 393220
  152.4 106.9 %all-reduce.3.cloned.1.call-start = ((), (), s32[]{:S(2)}) async-start(), calls=%async_computation.3 | async-start | bytes 4587520 | tf_op jit(solution)/shard_map/psum | solution.py:66
  153.3 8.0 %copy-start.4 = (f32[2,1,256,256]{3,2,1,0:T(8,128)S(1)}, f32[2,1,256,256]{3,2,1,0:T(8,128)}, u32[]{:S(2)}) copy-start(f32[2,1,256,256]{3,2,1,0:T(8,128)} %param.13) | copy-start | bytes 1572868
  180.2 3.7 %copy-start.1 = (f32[2,1024,512]{1,2,0:T(8,128)S(1)}, f32[2,1024,512]{1,2,0:T(8,128)}, u32[]{:S(2)}) copy-start(f32[2,1024,512]{1,2,0:T(8,128)} %all-gather.6.cloned.1.call-done) | copy-start | bytes 12582916
  184.0 4.7 %copy-start.3 = (f32[2,256,256]{2,1,0:T(8,128)S(1)}, f32[2,256,256]{2,1,0:T(8,128)}, u32[]{:S(2)}) copy-start(f32[2,256,256]{2,1,0:T(8,128)} %convolution_add_fusion.1) | copy-start | bytes 1572868
  259.3 2.6 copy-start.10
  259.3 3.3 %copy-start.8 = (f32[1,1024,64]{1,2,0:T(8,128)S(1)}, f32[1,1024,64]{1,2,0:T(8,128)}, u32[]{:S(2)}) copy-start(f32[1,1024,64]{1,2,0:T(8,128)} %get-tuple-element.27) | copy-start | bytes 786436
  259.3 4.0 %copy-start.9 = (f32[1,64,512]{2,1,0:T(8,128)S(1)}, f32[1,64,512]{2,1,0:T(8,128)}, u32[]{:S(2)}) copy-start(f32[1,64,512]{2,1,0:T(8,128)} %get-tuple-element.28) | copy-start | bytes 393220
  259.3 4.6 %copy-start.5 = (f32[1,512,256]{2,1,0:T(8,128)S(1)}, f32[1,512,256]{2,1,0:T(8,128)}, u32[]{:S(2)}) copy-start(f32[1,512,256]{2,1,0:T(8,128)} %get-tuple-element.30) | copy-start | bytes 1572868
  259.3 5.4 %copy-start.7 = (f32[1,256,256]{2,1,0:T(8,128)S(1)}, f32[1,256,256]{2,1,0:T(8,128)}, u32[]{:S(2)}) copy-start(f32[1,256,256]{2,1,0:T(8,128)} %get-tuple-element.31) | copy-start | bytes 786436
Sparse Core Ops, SparseCore 0:
  10.8 87.1 all-gather.3
  112.6 31.8 all-gather.5
  152.5 27.6 all-gather.7
  191.4 67.8 all-reduce.2
where the time goes:
time: 272 us
  waiting for transfers between devices  202 us (74%)
  matrix products  41 us (15%)
  between operations  13.9 us (5%)
  local copies, waits for them, and re-layouts  10.7 us (4%)
  other arithmetic  4.09 us (2%)
    all_gather x1, waiting for transfers between devices, shards(): lax.all_gather(root_inverse, ('row', 'col'), axis=1, tiled=True)  85.2 us
    psum x1, waiting for transfers between devices, shards(): lax.psum((upper_levels[0], upper_levels[1], upper_levels[2], leaf_levels[...  68 us
    dot_general x7, matrix products, product(): return jnp.matmul(left, right, precision=highest)  41 us
    all_gather x1, waiting for transfers between devices, shards(): piece = lax.all_gather(offdiag, 'col', axis=2, tiled=True)  31.9 us
    all_gather x1, waiting for transfers between devices, shards(): lax.all_gather(diag_rows, 'col', axis=1, tiled=True)  16 us
    unnamed x33, local copies, waits for them, and re-layouts  10.6 us
  transfers between devices with their start and end apart: 4, of which 4 were waited for; matrix products, arithmetic and copies ran while one was open for 6% of the time, Pallas kernels for 0%

commit v1 on v0

--- a/solution.py
+++ b/solution.py
@@ -4,6 +4,12 @@
 from jax.sharding import PartitionSpec as P
 
 highest = lax.Precision.HIGHEST
+
+
+def define_vectors_in(panel):
+    z2 = jnp.concatenate([panel] * jax.lax.axis_size("col"), 2)
+    field_out = jax.lax.all_to_all(z2, "col", 2, 2, tiled=True)
+    return field_out
 
 
 def product(left, right):
@@ -39,7 +45,7 @@
     col_index = lax.axis_index("col")
     own_rows = lax.dynamic_slice_in_dim(node_inv, col_index * width, width, 1)
     factor_t = jnp.swapaxes(node_cols, 1, 2)
-    piece = lax.all_gather(offdiag, "col", axis=2, tiled=True)
+    piece = define_vectors_in(offdiag)
     root_sum = root_times
     root_sum = root_sum + product(piece, node_leaf)
     node_part = product(jnp.swapaxes(piece, 1, 2), root_leaf)

time: 272 us -> 302 us (1.11)
  waiting for transfers between devices: 202 us -> 215 us
  local copies, waits for them, and re-layouts: 10.7 us -> 17.4 us
  matrix products: 41 us -> 46.7 us
  starting transfers between devices: 0.34 us -> 4.81 us
    all_to_all x0 -> x1, waiting for transfers between devices: none -> 48.8 us  [define_vectors_in(): field_out = jax.lax.all_to_all(z2, 'col', 2, 2, tiled=True)]
    all_gather x1 -> x0, waiting for transfers between devices: 31.9 us -> none  [shards(): piece = lax.all_gather(offdiag, 'col', axis=2, tiled=True)]
    dot_general x7, matrix products: 41 us -> 46.7 us  [product(): return jnp.matmul(left, right, precision=highest)]
    concatenate x0 -> x1, local copies, waits for them, and re-layouts: none -> 5.21 us  [define_vectors_in(): z2 = jnp.concatenate([panel] * jax.lax.axis_size('col'), 2)]
    all_to_all x0 -> x1, starting transfers between devices: none -> 4.67 us  [define_vectors_in(): field_out = jax.lax.all_to_all(z2, 'col', 2, 2, tiled=True)]
    all_gather x1, waiting for transfers between devices: 16 us -> 12.6 us  [shards(): lax.all_gather(diag_rows, 'col', axis=1, tiled=True)]
    unnamed x33 -> x27, local copies, waits for them, and re-layouts: 10.6 us -> 12.1 us
where the time goes in v1:
time: 302 us
  waiting for transfers between devices  215 us (71%)
  matrix products  46.7 us (15%)
  local copies, waits for them, and re-layouts  17.4 us (6%)
  between operations  13.9 us (5%)
  starting transfers between devices  4.81 us (2%)
  other arithmetic  3.64 us (1%)
    all_gather x1, waiting for transfers between devices, shards(): lax.all_gather(root_inverse, ('row', 'col'), axis=1, tiled=True)  85.3 us
    psum x1, waiting for transfers between devices, shards(): lax.psum((upper_levels[0], upper_levels[1], upper_levels[2], leaf_levels[...  68 us
    all_to_all x1, waiting for transfers between devices, define_vectors_in(): field_out = jax.lax.all_to_all(z2, 'col', 2, 2, tiled=True)  48.8 us
    dot_general x7, matrix products, product(): return jnp.matmul(left, right, precision=highest)  46.7 us
    all_gather x1, waiting for transfers between devices, shards(): lax.all_gather(diag_rows, 'col', axis=1, tiled=True)  12.6 us
    unnamed x27, local copies, waits for them, and re-layouts  12.1 us
  transfers between devices with their start and end apart: 4, of which 4 were waited for; matrix products, arithmetic and copies ran while one was open for 6% of the time, Pallas kernels for 0%

profile of v1, /device:TPU:1, one launch (start us, length us, event | category | flops | bytes accessed | tf_op | source)
XLA Modules:
  0.0 301.9 jit_solution(15523009197648540016)
XLA Ops:
  7.2 0.0 copy-start
  7.2 0.0 copy-start.9
  7.2 0.0 all-gather.3.cloned.1.call-start
  7.2 0.7 all-gather.3.cloned.1.call-update
  7.9 2.9 copy.22
  10.9 0.0 copy-done.9
  10.9 0.1 broadcast_bitcast_fusion
  10.9 1.8 bitcast_multiply_fusion
  12.8 85.3 %all-gather.3.cloned.1.call-done = f32[2,1024,1024]{2,1,0:T(8,128)} async-done(((f32[2,16,1024]{2,1,0:T(8,128)}), f32[2,1024,1024]{2,1,0:T(8,128)}) %all-gather.3.cloned.1.call-update) | async-done | bytes 8388624 | tf_op jit(solution)/shard_map/all_gather | solution.py:42
  98.0 11.3 %fusion.10 = f32[2,1024,320]{1,2,0:T(8,128)S(1)} fusion(f32[2,1024,1024]{2,1,0:T(8,128)} %all-gather.3.cloned.1.call-done, f32[2,1024,256]{1,2,0:T(8,128)S(1)} %bitcast_multiply_fusion, f32[2,1024,64]{1,2,0:T(8,128)} %bitcast.51), kind=kOutput, calls=%fused_computation.13 | convolution fusion | flops 8053719040 | bytes 13631488 | tf_op jit(solution)/shard_map/dot_general | solution.py:16
  109.4 0.0 copy-start.1
  109.5 0.0 copy-start.8
  109.7 1.2 copy-done.1
  110.9 0.0 copy-done.8
  110.9 0.8 fusion.38
  111.8 5.2 %copy.23 = f32[2,1024,512]{1,0,2:T(2,128)} copy(f32[2,1024,512]{1,2,0:T(8,128)S(1)} %get-tuple-element.18) | data formatting | bytes 8388608 | tf_op jit(solution)/shard_map/concatenate | solution.py:10
  117.0 4.7 %all-to-all-start = ((f32[2,1024,512]{1,0,2:T(2,128)}), f32[2,1024,512]{1,0,2:T(2,128)}, u32[]{:S(2)}, u32[]{:S(2)}) async-start(f32[2,1024,512]{1,0,2:T(2,128)} %copy.23), calls=%async_computation | async-start | bytes 8388608 | tf_op jit(solution)/shard_map/all_to_all | solution.py:11
  121.7 0.1 all-gather.5.cloned.1.call-start
  121.7 0.0 copy-start.5
  121.7 48.8 %all-to-all-done = f32[2,1024,512]{1,0,2:T(2,128)} async-done(((f32[2,1024,512]{1,0,2:T(2,128)}), f32[2,1024,512]{1,0,2:T(2,128)}, u32[]{:S(2)}, u32[]{:S(2)}) %all-to-all-start) | async-done | bytes 4194336 | tf_op jit(solution)/shard_map/all_to_all | solution.py:11
  170.6 8.9 %multiply_reduce_fusion.3 = (f32[64,512]{1,0:T(8,128)}, f32[2,64,512]{2,1,0:T(8,128)}) fusion(f32[2]{0:T(128)S(1)} %copy-done.8, f32[2,1,1024,64]{2,3,1,0:T(8,128)} %param.9, f32[2,1024,512]{1,0,2:T(2,128)} %all-to-all-done, f32[2,1,512,512]{3,2,1,0:T(8,128)} %param.10, s32[]{:T(128)S(6)} %select_n.3), kind=kOutput, calls=%fused_computation.29 | convolution fusion | flops 805470208 | bytes 5373964 | tf_op jit(solution)/shard_map/dot_general | solution.py:16
  179.5 0.0 all-gather.5.cloned.1.call-update
  179.6 0.0 all-reduce.3.cloned.1.call-start
  179.6 0.0 copy-done.5
  179.6 0.7 multiply_reduce_fusion.4
  180.3 0.0 copy-done
  180.3 0.0 copy-start.3
  180.3 9.1 %multiply_reduce_fusion = (f32[1024,256]{0,1:T(8,128)}, f32[2,1024,256]{1,2,0:T(8,128)S(1)}) fusion(f32[2]{0:T(128)S(1)} %copy-done.8, f32[2,1,512,256]{3,2,1,0:T(8,128)S(1)} %copy-done, f32[2,1024,512]{1,0,2:T(2,128)} %all-to-all-done, f32[2,1024,320]{1,2,0:T(8,128)} %copy-done.1), kind=kOutput, calls=%fused_computation.12 | convolution fusion | flops 3223060480 | bytes 10485768 | tf_op jit(solution)/shard_map/dot_general | solution.py:16
  189.4 0.0 copy-done.3
  189.4 2.9 convolution_add_fusion
  192.4 12.6 %all-gather.5.cloned.1.call-done = f32[2,512,512]{2,1,0:T(8,128)} async-done(((f32[2,64,512]{2,1,0:T(8,128)}), f32[2,512,512]{2,1,0:T(8,128)}) %all-gather.5.cloned.1.call-update) | async-done | bytes 2097168 | tf_op jit(solution)/shard_map/all_gather | solution.py:55
  204.9 3.6 %fusion.28 = f32[2,512,256]{2,1,0:T(8,128)S(1)} fusion(f32[2,512,512]{2,1,0:T(8,128)} %all-gather.5.cloned.1.call-done, f32[2,1,512,256]{3,2,1,0:T(8,128)S(1)} %copy-done), kind=kOutput, calls=%fused_computation.23 | convolution fusion | flops 1610612736 | bytes 4194304 | tf_op jit(solution)/shard_map/dot_general | solution.py:16
  208.5 0.0 copy-start.2
  208.5 8.3 %multiply_reduce_fusion.1 = (f32[512,256]{1,0:T(8,128)}, f32[2,512,256]{2,1,0:T(8,128)S(1)}) fusion(f32[2]{0:T(128)S(1)} %copy-done.8, f32[2,512,256]{2,1,0:T(8,128)S(1)} %fusion.28, f32[2,1024,256]{1,2,0:T(8,128)S(1)} %bitcast_multiply_fusion, f32[2,1024,512]{1,0,2:T(2,128)} %all-to-all-done), kind=kOutput, calls=%fused_computation.26 | convolution fusion | flops 3222142976 | bytes 8912904 | tf_op jit(solution)/shard_map/dot_general | solution.py:16
  216.8 0.0 copy-done.2
  216.8 2.6 fusion.20
  219.4 0.0 all-reduce.3.cloned.1.call-update
  219.4 68.0 %all-reduce.3.cloned.1.call-done = (f32[16,1024]{1,0:T(8,128)}, f32[1,1024,64]{1,2,0:T(8,128)}, f32[1,64,512]{2,1,0:T(8,128)}, f32[1,1024,256]{1,2,0:T(8,128)}, ...) async-done(((f32[16,1024]{1,0:T(8,128)}, f32[1,1024,64]{1,2,0:T(8,128)}, f32[1,64,512]{2,1,0:T(8,128)}, f32[1,1024,256]{1,2,0:T(8,128)}, f32[1,512,256]{2,1,0:T(8,128)}, ...) | async-done | bytes 2293776 | tf_op jit(solution)/shard_map/psum | solution.py:72
  287.4 0.0 copy-start.7
  287.4 2.6 copy.32
  290.0 1.5 copy.71
  291.5 1.7 copy.72
  293.2 0.0 copy-done.7
  293.2 0.7 copy.73
  293.8 0.0 copy-done.4
  293.8 0.8 copy.74
  294.6 0.0 copy-done.6
  294.6 0.7 copy.75
  (10 shorter events, 0.3 us)
Async XLA Ops:
  7.2 173.2 %copy-start = (f32[2,1,512,256]{3,2,1,0:T(8,128)S(1)}, f32[2,1,512,256]{3,2,1,0:T(8,128)}, u32[]{:S(2)}) copy-start(f32[2,1,512,256]{3,2,1,0:T(8,128)} %param.12) | copy-start | bytes 3145732
  7.2 3.7 %copy-start.9 = (s32[1,8]{1,0:T(1,128)S(1)}, s32[1,8]{1,0:T(1,128)}, u32[]{:S(2)}) copy-start(s32[1,8]{1,0:T(1,128)} %param.14) | copy-start | bytes 100
  7.2 90.8 %all-gather.3.cloned.1.call-start = ((), (), s32[]{:S(2)}) async-start(), calls=%async_computation.1 | async-start | bytes 8519680 | tf_op jit(solution)/shard_map/all_gather | solution.py:42
  109.4 1.6 copy-start.1
  109.5 1.5 copy-start.8
  117.0 53.6 %all-to-all-start = ((f32[2,1024,512]{1,0,2:T(2,128)}), f32[2,1024,512]{1,0,2:T(2,128)}, u32[]{:S(2)}, u32[]{:S(2)}) async-start(f32[2,1024,512]{1,0,2:T(2,128)} %copy.23), calls=%async_computation | async-start | bytes 8388608 | tf_op jit(solution)/shard_map/all_to_all | solution.py:11
  121.7 83.3 %all-gather.5.cloned.1.call-start = ((), (), s32[]{:S(2)}) async-start(), calls=%async_computation.2 | async-start | bytes 2359296 | tf_op jit(solution)/shard_map/all_gather | solution.py:55
  121.7 57.9 %copy-start.5 = (f32[2,16,1024]{2,1,0:T(8,128)S(1)}, f32[2,16,1024]{2,1,0:T(8,128)}, u32[]{:S(2)}) copy-start(f32[2,16,1024]{2,1,0:T(8,128)} %param.8) | copy-start | bytes 393220
  179.6 107.9 %all-reduce.3.cloned.1.call-start = ((), (), s32[]{:S(2)}) async-start(), calls=%async_computation.3 | async-start | bytes 4587520 | tf_op jit(solution)/shard_map/psum | solution.py:72
  180.3 9.1 %copy-start.3 = (f32[2,1,256,256]{3,2,1,0:T(8,128)S(1)}, f32[2,1,256,256]{3,2,1,0:T(8,128)}, u32[]{:S(2)}) copy-start(f32[2,1,256,256]{3,2,1,0:T(8,128)} %param.13) | copy-start | bytes 1572868
  208.5 8.3 %copy-start.2 = (f32[2,256,256]{2,1,0:T(8,128)S(1)}, f32[2,256,256]{2,1,0:T(8,128)}, u32[]{:S(2)}) copy-start(f32[2,256,256]{2,1,0:T(8,128)} %convolution_add_fusion) | copy-start | bytes 1572868
  287.4 5.8 %copy-start.7 = (f32[1,64,512]{2,1,0:T(8,128)S(1)}, f32[1,64,512]{2,1,0:T(8,128)}, u32[]{:S(2)}) copy-start(f32[1,64,512]{2,1,0:T(8,128)} %get-tuple-element.28) | copy-start | bytes 393220
  287.4 6.4 %copy-start.4 = (f32[1,512,256]{2,1,0:T(8,128)S(1)}, f32[1,512,256]{2,1,0:T(8,128)}, u32[]{:S(2)}) copy-start(f32[1,512,256]{2,1,0:T(8,128)} %get-tuple-element.30) | copy-start | bytes 1572868
  287.4 7.2 %copy-start.6 = (f32[1,256,256]{2,1,0:T(8,128)S(1)}, f32[1,256,256]{2,1,0:T(8,128)}, u32[]{:S(2)}) copy-start(f32[1,256,256]{2,1,0:T(8,128)} %get-tuple-element.31) | copy-start | bytes 786436
Sparse Core Ops, SparseCore 0:
  10.8 87.1 all-gather.2
  179.7 25.2 all-gather.4
  219.5 67.8 all-reduce.2
